TPU v7x, 32 devices: a whole 2x2x4 slice. The times are simulated.
32 devices in a mesh: prow: 4 (over y, core), pcol: 8 (over z, x).
Axes of the slice: x: 2, y: 2, z: 4, core: 2. Of those that a mesh axis runs over, the one named last changes fastest.
Arguments:
- right_side: float32 [8, 256, 128], P(None, 'prow'), may hold values from -6 to 6
- lower_prev: float32 [8, 256, 129024], P(None, 'prow', 'pcol'), may hold values from -0.015625 to 0.015625
- solved_prev: float32 [129024, 128], P('pcol'), may hold values from -6 to 6
- lower_window: float32 [8, 256, 2048], P(None, 'prow', 'pcol'), may hold values from -0.1875 to 0.1875
- inverse_diag: float32 [8, 256, 256], P(None, 'prow'), may hold values from -0.25 to 1.4, as said below
Outputs:
- solution: float32 [8, 256, 128], P(None, 'prow')
Inputs may be any that keep to these rules, and one draw needn't show every extreme that they name: `inverse_diag`: each block is lower triangular: zero above its diagonal, with diagonal entries of 0.7 to 1.4.
All inputs are finite; a program needn't handle non-finite values.
Results may differ from a plain program's by a relative error of at most 0.00011.
Values sent between devices are 32-bit elements; how exact they have to be, the bound alone decides.
No kernel may reach another device: no remote copies, remote signals or barrier semaphores. Data moves between devices by JAX's collectives and lax.ppermute only.
A program may use at most 128 MiB of HBM per device.

v0:
```python
import jax
import jax.numpy as jnp
from jax import lax
from jax.sharding import PartitionSpec as P


def local(right_side, lower_prev, solved_prev, lower_window, inverse_diag):
    highest = lax.Precision.HIGHEST
    blocks = right_side.shape[0]
    local_rows = right_side.shape[1]
    columns = right_side.shape[2]
    block_rows = inverse_diag.shape[2]
    row_start = lax.axis_index("prow") * local_rows
    solved = jnp.zeros((blocks * block_rows, columns), jnp.float32)
    pieces = []
    full_inverse = lax.all_gather(inverse_diag, "prow", axis=1, tiled=True)
    full_window = lax.all_gather(lower_window, "pcol", axis=2, tiled=True)
    for row_block in range(blocks):
        window_term = jnp.dot(
            full_window[row_block], solved, precision=highest, preferred_element_type=jnp.float32
        )
        earlier_part = jnp.dot(
            lower_prev[row_block],
            solved_prev,
            precision=highest,
            preferred_element_type=jnp.float32,
        )
        earlier_here = lax.psum(earlier_part, "pcol")
        local_residual = right_side[row_block] - (earlier_here + window_term)
        residual = lax.all_gather(local_residual, "prow", axis=0, tiled=True)
        whole_rows = jnp.dot(
            full_inverse[row_block], residual, precision=highest, preferred_element_type=jnp.float32
        )
        pieces.append(lax.dynamic_slice_in_dim(whole_rows, row_start, local_rows, 0))
        solved = lax.dynamic_update_slice_in_dim(solved, whole_rows, row_block * block_rows, 0)
    return jnp.stack(pieces)


def solution(mesh):
    in_specs = (
        P(None, "prow", None),
        P(None, "prow", "pcol"),
        P("pcol", None),
        P(None, "prow", "pcol"),
        P(None, "prow", None),
    )
    out_specs = P(None, "prow", None)
    return jax.shard_map(local, mesh=mesh, in_specs=in_specs, out_specs=out_specs, check_vma=False)
```

profile of v0, /device:TPU:0, one launch (start us, length us, event | category | flops | bytes accessed | tf_op | source)
XLA Modules:
  0.0 249.5 jit_solution(15784132453054589347)
XLA Ops:
  7.3 10.3 %fusion.4 = f32[64,128]{1,0:T(8,128)} fusion(f32[16128,128]{1,0:T(8,128)} %param.7, f32[8,64,16128]{2,1,0:T(8,128)} %param.6), kind=kOutput, calls=%fused_computation.4 | convolution fusion | flops 1585446912 | bytes 12419072 | tf_op jit(solution)/shard_map/dot_general | solution.py:22
  17.7 8.1 %fusion.6 = f32[64,128]{1,0:T(8,128)} fusion(f32[16128,128]{1,0:T(8,128)S(1)} %copy-done, f32[8,64,16128]{2,1,0:T(8,128)} %param.6), kind=kOutput, calls=%fused_computation.6 | convolution fusion | flops 1585446912 | bytes 12419072 | tf_op jit(solution)/shard_map/dot_general | solution.py:22
  25.8 7.9 %fusion.8 = f32[64,128]{1,0:T(8,128)} fusion(f32[16128,128]{1,0:T(8,128)S(1)} %copy-done, f32[8,64,16128]{2,1,0:T(8,128)} %param.6), kind=kOutput, calls=%fused_computation.8 | convolution fusion | flops 1585446912 | bytes 12419072 | tf_op jit(solution)/shard_map/dot_general | solution.py:22
  33.7 8.1 %fusion.10 = f32[64,128]{1,0:T(8,128)} fusion(f32[16128,128]{1,0:T(8,128)S(1)} %copy-done, f32[8,64,16128]{2,1,0:T(8,128)} %param.6), kind=kOutput, calls=%fused_computation.10 | convolution fusion | flops 1585446912 | bytes 12419072 | tf_op jit(solution)/shard_map/dot_general | solution.py:22
  41.8 7.9 %fusion.12 = f32[64,128]{1,0:T(8,128)} fusion(f32[16128,128]{1,0:T(8,128)S(1)} %copy-done, f32[8,64,16128]{2,1,0:T(8,128)} %param.6), kind=kOutput, calls=%fused_computation.12 | convolution fusion | flops 1585446912 | bytes 12419072 | tf_op jit(solution)/shard_map/dot_general | solution.py:22
  49.7 8.4 %fusion.14 = f32[64,128]{1,0:T(8,128)} fusion(f32[16128,128]{1,0:T(8,128)S(1)} %copy-done, f32[8,64,16128]{2,1,0:T(8,128)} %param.6), kind=kOutput, calls=%fused_computation.14 | convolution fusion | flops 1585446912 | bytes 12419072 | tf_op jit(solution)/shard_map/dot_general | solution.py:22
  58.1 7.9 %fusion = f32[64,128]{1,0:T(8,128)} fusion(f32[16128,128]{1,0:T(8,128)S(1)} %copy-done, f32[8,64,16128]{2,1,0:T(8,128)} %param.6), kind=kOutput, calls=%fused_computation | convolution fusion | flops 1585446912 | bytes 12419072 | tf_op jit(solution)/shard_map/dot_general | solution.py:22
  66.1 8.2 %fusion.2 = f32[64,128]{1,0:T(8,128)} fusion(f32[16128,128]{1,0:T(8,128)S(1)} %copy-done, f32[8,64,16128]{2,1,0:T(8,128)} %param.6), kind=kOutput, calls=%fused_computation.2 | convolution fusion | flops 1585446912 | bytes 12419072 | tf_op jit(solution)/shard_map/dot_general | solution.py:22
  75.0 12.2 %all-gather.3.cloned.1.call-done = f32[8,64,2048]{2,1,0:T(8,128)} async-done(((f32[8,64,256]{2,1,0:T(8,128)}), f32[8,64,2048]{2,1,0:T(8,128)}) %all-gather.3.cloned.1.call-update) | async-done | bytes 4194320 | tf_op jit(solution)/shard_map/all_gather | solution.py:17
  88.3 73.8 %all-reduce.4.cloned.1.call-done = (f32[64,128]{1,0:T(8,128)}, f32[64,128]{1,0:T(8,128)}, f32[64,128]{1,0:T(8,128)}, f32[64,128]{1,0:T(8,128)}, f32[64,128]{1,0:...) async-done(((f32[64,128]{1,0:T(8,128)}, f32[64,128]{1,0:T(8,128)}, f32[64,128]{1,0:T(8,128)}, f32[64,128]{1,0:T(8,128)}, f32[64,128]{1,0:T(8,128)}, ...) | async-done | bytes 262160 | tf_op jit(solution)/shard_map/psum | solution.py:28
  163.0 5.4 %all_gather.31 = f32[256,128]{1,0:T(8,128)S(1)} all-gather(f32[64,128]{1,0:T(8,128)S(1)} %bitcast_subtract_fusion), channel_id=1, replica_groups=mesh['prow'=4,'pcol'=8] {'prow'}, dimensions={0}, use_global_device_ids=true | all-gather | bytes 163840 | tf_op jit(solution)/shard_map/all_gather | solution.py:30
  168.4 17.4 %all-gather.5.cloned.1.call-done = f32[8,256,256]{2,1,0:T(8,128)} async-done(((f32[8,64,256]{2,1,0:T(8,128)}), f32[8,256,256]{2,1,0:T(8,128)}) %all-gather.5.cloned.1.call-update) | async-done | bytes 2097168 | tf_op jit(solution)/shard_map/all_gather | solution.py:16
  185.8 1.5 fusion.47
  187.3 2.1 fusion.25
  189.4 5.4 %all_gather.33 = f32[256,128]{1,0:T(8,128)S(1)} all-gather(f32[64,128]{1,0:T(8,128)S(1)} %fusion.25), channel_id=1, replica_groups=mesh['prow'=4,'pcol'=8] {'prow'}, dimensions={0}, use_global_device_ids=true | all-gather | bytes 163840 | tf_op jit(solution)/shard_map/all_gather | solution.py:30
  195.0 1.4 bitcast_dynamic-update-slice_fusion.5
  196.4 2.3 fusion.27
  198.7 5.4 %all_gather.34 = f32[256,128]{1,0:T(8,128)S(1)} all-gather(f32[64,128]{1,0:T(8,128)S(1)} %fusion.27), channel_id=1, replica_groups=mesh['prow'=4,'pcol'=8] {'prow'}, dimensions={0}, use_global_device_ids=true | all-gather | bytes 163840 | tf_op jit(solution)/shard_map/all_gather | solution.py:30
  204.1 1.4 bitcast_dynamic-update-slice_fusion.4
  206.7 5.6 %all_gather.35 = f32[256,128]{1,0:T(8,128)S(1)} all-gather(f32[64,128]{1,0:T(8,128)S(1)} %fusion.29), channel_id=1, replica_groups=mesh['prow'=4,'pcol'=8] {'prow'}, dimensions={0}, use_global_device_ids=true | all-gather | bytes 163840 | tf_op jit(solution)/shard_map/all_gather | solution.py:30
  213.9 5.4 %all_gather.36 = f32[256,128]{1,0:T(8,128)S(1)} all-gather(f32[64,128]{1,0:T(8,128)S(1)} %fusion.31), channel_id=1, replica_groups=mesh['prow'=4,'pcol'=8] {'prow'}, dimensions={0}, use_global_device_ids=true | all-gather | bytes 163840 | tf_op jit(solution)/shard_map/all_gather | solution.py:30
  221.0 5.4 %all_gather.37 = f32[256,128]{1,0:T(8,128)S(1)} all-gather(f32[64,128]{1,0:T(8,128)S(1)} %fusion.33), channel_id=1, replica_groups=mesh['prow'=4,'pcol'=8] {'prow'}, dimensions={0}, use_global_device_ids=true | all-gather | bytes 163840 | tf_op jit(solution)/shard_map/all_gather | solution.py:30
  228.1 5.6 %all_gather.38 = f32[256,128]{1,0:T(8,128)S(1)} all-gather(f32[64,128]{1,0:T(8,128)S(1)} %fusion.35), channel_id=1, replica_groups=mesh['prow'=4,'pcol'=8] {'prow'}, dimensions={0}, use_global_device_ids=true | all-gather | bytes 163840 | tf_op jit(solution)/shard_map/all_gather | solution.py:30
  235.4 5.4 %all_gather.39 = f32[256,128]{1,0:T(8,128)S(1)} all-gather(f32[64,128]{1,0:T(8,128)S(1)} %fusion.37), channel_id=1, replica_groups=mesh['prow'=4,'pcol'=8] {'prow'}, dimensions={0}, use_global_device_ids=true | all-gather | bytes 163840 | tf_op jit(solution)/shard_map/all_gather | solution.py:30
  (46 shorter events, 13.4 us)
Async XLA Ops:
  6.5 80.6 %all-gather.3.cloned.1.call-start = ((), (), s32[]{:S(2)}) async-start(), calls=%async_computation | async-start | bytes 4718592 | tf_op jit(solution)/shard_map/all_gather | solution.py:17
  7.3 154.9 %all-reduce.4.cloned.1.call-start = ((), (), s32[]{:S(2)}) async-start(), calls=%async_computation.2 | async-start | bytes 524288 | tf_op jit(solution)/shard_map/psum | solution.py:28
  7.3 10.4 %copy-start = (f32[16128,128]{1,0:T(8,128)S(1)}, f32[16128,128]{1,0:T(8,128)}, u32[]{:S(2)}) copy-start(f32[16128,128]{1,0:T(8,128)} %param.7) | copy-start | bytes 24772612
  66.1 96.1 %copy-start.3 = (f32[8,64,128]{2,1,0:T(8,128)S(1)}, f32[8,64,128]{2,1,0:T(8,128)}, u32[]{:S(2)}) copy-start(f32[8,64,128]{2,1,0:T(8,128)} %param.5) | copy-start | bytes 786436
  74.2 111.6 %all-gather.5.cloned.1.call-start = ((), (), s32[]{:S(2)}) async-start(), calls=%async_computation.1 | async-start | bytes 2621440 | tf_op jit(solution)/shard_map/all_gather | solution.py:16
  162.1 43.4 %copy-start.8 = (f32[64,128]{1,0:T(8,128)S(1)}, f32[64,128]{1,0:T(8,128)}, u32[]{:S(2)}) copy-start(f32[64,128]{1,0:T(8,128)} %get-tuple-element.8) | copy-start | bytes 98308
  168.4 44.3 %copy-start.7 = (f32[64,128]{1,0:T(8,128)S(1)}, f32[64,128]{1,0:T(8,128)}, u32[]{:S(2)}) copy-start(f32[64,128]{1,0:T(8,128)} %get-tuple-element.9) | copy-start | bytes 98308
  185.8 19.7 %copy-start.1 = (f32[8,64,2048]{2,1,0:T(8,128)S(1)}, f32[8,64,2048]{2,1,0:T(8,128)}, u32[]{:S(2)}) copy-start(f32[8,64,2048]{2,1,0:T(8,128)} %all-gather.3.cloned.1.call-done) | copy-start | bytes 12582916
  185.8 26.5 %copy-start.2 = (f32[8,256,256]{2,1,0:T(8,128)S(1)}, f32[8,256,256]{2,1,0:T(8,128)}, u32[]{:S(2)}) copy-start(f32[8,256,256]{2,1,0:T(8,128)} %all-gather.5.cloned.1.call-done) | copy-start | bytes 6291460
  195.0 24.8 %copy-start.6 = (f32[64,128]{1,0:T(8,128)S(1)}, f32[64,128]{1,0:T(8,128)}, u32[]{:S(2)}) copy-start(f32[64,128]{1,0:T(8,128)} %get-tuple-element.10) | copy-start | bytes 98308
  198.7 28.2 %copy-start.5 = (f32[64,128]{1,0:T(8,128)S(1)}, f32[64,128]{1,0:T(8,128)}, u32[]{:S(2)}) copy-start(f32[64,128]{1,0:T(8,128)} %get-tuple-element.11) | copy-start | bytes 98308
  206.7 27.4 %copy-start.4 = (f32[64,128]{1,0:T(8,128)S(1)}, f32[64,128]{1,0:T(8,128)}, u32[]{:S(2)}) copy-start(f32[64,128]{1,0:T(8,128)} %get-tuple-element.12) | copy-start | bytes 98308
Sparse Core Ops, SparseCore 0:
  9.4 77.7 all-gather.2
  91.4 70.6 all-reduce.3
  163.8 21.9 all-gather.4
where the time goes:
time: 253 us; the launch traced here: 249 us
  waiting for transfers between devices  105 us (42%)
  matrix products  83.6 us (33%)
  blocking collectives  43.7 us (17%)
  between operations  13.6 us (5%)
    psum x1, waiting for transfers between devices, local(): earlier_here = lax.psum(earlier_part, 'pcol')  73.8 us
    dot_general x8, matrix products, local(): jnp.dot(lower_prev[row_block], solved_prev, precision=highest, preferred_...  66.9 us
    all_gather x8, blocking collectives, local(): residual = lax.all_gather(local_residual, 'prow', axis=0, tiled=True)  43.7 us
    all_gather x1, waiting for transfers between devices, local(): full_inverse = lax.all_gather(inverse_diag, 'prow', axis=1, tiled=True)  17.4 us
    all_gather x1, waiting for transfers between devices, local(): full_window = lax.all_gather(lower_window, 'pcol', axis=2, tiled=True)  12.2 us
    dot_general x7, matrix products, local(): jnp.dot(full_window[row_block], solved, precision=highest, preferred_elem...  10.4 us
    dot_general x8, matrix products, local(): jnp.dot(full_inverse[row_block], residual, precision=highest, preferred_e...  6.33 us
  transfers between devices with their start and end apart: 3, of which 3 were waited for; matrix products, arithmetic and copies ran while one was open for 28% of the time, Pallas kernels for 0%

commit v1 on v0

--- a/solution.py
+++ b/solution.py
@@ -13,7 +13,14 @@
     row_start = lax.axis_index("prow") * local_rows
     solved = jnp.zeros((blocks * block_rows, columns), jnp.float32)
     pieces = []
-    full_inverse = lax.all_gather(inverse_diag, "prow", axis=1, tiled=True)
+    size = lax.axis_size("prow")
+    right = [(i, (i + 1) % size) for i in range(size)]
+    parts = [inverse_diag]
+    for far in range(1, size):
+        parts = [lax.ppermute(parts[0], "prow", right), *parts]
+    result = jnp.concatenate(parts, axis=1)
+    shift = (lax.axis_index("prow") + 1) * parts[-1].shape[1]
+    full_inverse = jnp.roll(result, shift, axis=1)
     full_window = lax.all_gather(lower_window, "pcol", axis=2, tiled=True)
     for row_block in range(blocks):
         window_term = jnp.dot(

time: 253 us -> 237 us (0.937)
  waiting for transfers between devices: 105 us -> 77.1 us
  local copies, waits for them, and re-layouts: 1.71 us -> 8.32 us
  starting transfers between devices: 0.08 us -> 3.5 us
    all_gather x1 -> x0, waiting for transfers between devices: 17.4 us -> none  [local(): full_inverse = lax.all_gather(inverse_diag, 'prow', axis=1, tiled=True)]
    all_gather x1, waiting for transfers between devices: 12.2 us -> 2.17 us  [local(): full_window = lax.all_gather(lower_window, 'pcol', axis=2, tiled=True)]
    unnamed x25 -> x34, local copies, waits for them, and re-layouts: 0.64 us -> 6.77 us
    dot_general x8, matrix products: 6.33 us -> 10.6 us  [local(): jnp.dot(full_inverse[row_block], residual, precision=highest, preferred_e...]
    ppermute x0 -> x3, starting transfers between devices: none -> 3.46 us  [local(): parts = [lax.ppermute(parts[0], 'prow', right), *parts]]
    dot_general x7, matrix products: 10.4 us -> 7.35 us  [local(): jnp.dot(full_window[row_block], solved, precision=highest, preferred_elem...]
  transfers between devices with their start and end apart: 3 -> 5, of which waited for: 3 -> 3; matrix products, arithmetic and copies ran while one was open for 28% -> 32% of each run, Pallas kernels for 0% -> 0%
where the time goes in v1:
time: 237 us; the launch traced here: 233 us
  matrix products  84.8 us (36%)
  waiting for transfers between devices  77.1 us (33%)
  blocking collectives  43.7 us (18%)
  between operations  13.9 us (6%)
  local copies, waits for them, and re-layouts  8.32 us (4%)
  starting transfers between devices  3.5 us (1%)
    psum x1, waiting for transfers between devices, local(): earlier_here = lax.psum(earlier_part, 'pcol')  73.8 us
    dot_general x8, matrix products, local(): jnp.dot(lower_prev[row_block], solved_prev, precision=highest, preferred_...  66.8 us
    all_gather x8, blocking collectives, local(): residual = lax.all_gather(local_residual, 'prow', axis=0, tiled=True)  43.7 us
    dot_general x8, matrix products, local(): jnp.dot(full_inverse[row_block], residual, precision=highest, preferred_e...  10.6 us
    dot_general x7, matrix products, local(): jnp.dot(full_window[row_block], solved, precision=highest, preferred_elem...  7.35 us
    unnamed x34, local copies, waits for them, and re-layouts  6.77 us
  transfers between devices with their start and end apart: 5, of which 3 were waited for; matrix products, arithmetic and copies ran while one was open for 32% of the time, Pallas kernels for 0%

profile of v1, /device:TPU:0, one launch (start us, length us, event | category | flops | bytes accessed | tf_op | source)
XLA Modules:
  0.0 233.5 jit_solution(17388461550440783885)
XLA Ops:
  7.8 10.7 %fusion = f32[64,128]{1,0:T(8,128)} fusion(f32[16128,128]{1,0:T(8,128)} %param.7, f32[8,64,16128]{2,1,0:T(8,128)} %param.6), kind=kOutput, calls=%fused_computation | convolution fusion | flops 1585446912 | bytes 12419072 | tf_op jit(solution)/shard_map/dot_general | solution.py:29
  18.6 8.2 %fusion.10 = f32[64,128]{1,0:T(8,128)} fusion(f32[16128,128]{1,0:T(8,128)S(1)} %copy-done, f32[8,64,16128]{2,1,0:T(8,128)} %param.6), kind=kOutput, calls=%fused_computation.10 | convolution fusion | flops 1585446912 | bytes 12419072 | tf_op jit(solution)/shard_map/dot_general | solution.py:29
  26.7 7.9 %fusion.12 = f32[64,128]{1,0:T(8,128)} fusion(f32[16128,128]{1,0:T(8,128)S(1)} %copy-done, f32[8,64,16128]{2,1,0:T(8,128)} %param.6), kind=kOutput, calls=%fused_computation.12 | convolution fusion | flops 1585446912 | bytes 12419072 | tf_op jit(solution)/shard_map/dot_general | solution.py:29
  34.6 8.1 %fusion.14 = f32[64,128]{1,0:T(8,128)} fusion(f32[16128,128]{1,0:T(8,128)S(1)} %copy-done, f32[8,64,16128]{2,1,0:T(8,128)} %param.6), kind=kOutput, calls=%fused_computation.14 | convolution fusion | flops 1585446912 | bytes 12419072 | tf_op jit(solution)/shard_map/dot_general | solution.py:29
  42.8 7.9 %fusion.2 = f32[64,128]{1,0:T(8,128)} fusion(f32[16128,128]{1,0:T(8,128)S(1)} %copy-done, f32[8,64,16128]{2,1,0:T(8,128)} %param.6), kind=kOutput, calls=%fused_computation.2 | convolution fusion | flops 1585446912 | bytes 12419072 | tf_op jit(solution)/shard_map/dot_general | solution.py:29
  50.7 8.2 %fusion.4 = f32[64,128]{1,0:T(8,128)} fusion(f32[16128,128]{1,0:T(8,128)S(1)} %copy-done, f32[8,64,16128]{2,1,0:T(8,128)} %param.6), kind=kOutput, calls=%fused_computation.4 | convolution fusion | flops 1585446912 | bytes 12419072 | tf_op jit(solution)/shard_map/dot_general | solution.py:29
  58.9 2.4 %collective-permute-start.1 = (f32[8,64,256]{2,1,0:T(8,128)S(1)}, f32[8,64,256]{2,1,0:T(8,128)S(1)}, u32[]{:S(2)}, u32[]{:S(2)}) collective-permute-start(f32[8,64,256]{2,1,0:T(8,128)S(1)} %collective-permute-done), channel_id=1, source_target_pairs={{0,8},{8,16},{16,24},{24,0},{1,9},{9,17},{17,25},{25,1},{2,10},{10... | collective-permute-start | bytes 1572872 | tf_op jit(solution)/shard_map/ppermute | solution.py:20
  61.2 7.9 %fusion.6 = f32[64,128]{1,0:T(8,128)} fusion(f32[16128,128]{1,0:T(8,128)S(1)} %copy-done, f32[8,64,16128]{2,1,0:T(8,128)} %param.6), kind=kOutput, calls=%fused_computation.6 | convolution fusion | flops 1585446912 | bytes 12419072 | tf_op jit(solution)/shard_map/dot_general | solution.py:29
  69.7 7.9 %fusion.8 = f32[64,128]{1,0:T(8,128)} fusion(f32[16128,128]{1,0:T(8,128)S(1)} %copy-done, f32[8,64,16128]{2,1,0:T(8,128)} %param.6), kind=kOutput, calls=%fused_computation.8 | convolution fusion | flops 1585446912 | bytes 12419072 | tf_op jit(solution)/shard_map/dot_general | solution.py:29
  85.0 2.2 all-gather.2.cloned.1.call-done
  88.3 73.8 %all-reduce.4.cloned.1.call-done = (f32[64,128]{1,0:T(8,128)}, f32[64,128]{1,0:T(8,128)}, f32[64,128]{1,0:T(8,128)}, f32[64,128]{1,0:T(8,128)}, f32[64,128]{1,0:...) async-done(((f32[64,128]{1,0:T(8,128)}, f32[64,128]{1,0:T(8,128)}, f32[64,128]{1,0:T(8,128)}, f32[64,128]{1,0:T(8,128)}, f32[64,128]{1,0:T(8,128)}, ...) | async-done | bytes 262160 | tf_op jit(solution)/shard_map/psum | solution.py:35
  163.1 5.6 %all_gather.28 = f32[256,128]{1,0:T(8,128)S(1)} all-gather(f32[64,128]{1,0:T(8,128)S(1)} %bitcast_subtract_fusion), channel_id=1, replica_groups=mesh['prow'=4,'pcol'=8] {'prow'}, dimensions={0}, use_global_device_ids=true | all-gather | bytes 163840 | tf_op jit(solution)/shard_map/all_gather | solution.py:37
  170.1 1.6 fusion.25
  171.7 5.4 %all_gather.29 = f32[256,128]{1,0:T(8,128)S(1)} all-gather(f32[64,128]{1,0:T(8,128)S(1)} %fusion.25), channel_id=1, replica_groups=mesh['prow'=4,'pcol'=8] {'prow'}, dimensions={0}, use_global_device_ids=true | all-gather | bytes 163840 | tf_op jit(solution)/shard_map/all_gather | solution.py:37
  177.1 1.3 constant_dynamic-update-slice_fusion.21
  178.5 1.8 fusion.27
  180.3 5.4 %all_gather.30 = f32[256,128]{1,0:T(8,128)S(1)} all-gather(f32[64,128]{1,0:T(8,128)S(1)} %fusion.27), channel_id=1, replica_groups=mesh['prow'=4,'pcol'=8] {'prow'}, dimensions={0}, use_global_device_ids=true | all-gather | bytes 163840 | tf_op jit(solution)/shard_map/all_gather | solution.py:37
  185.7 1.3 constant_dynamic-update-slice_fusion.20
  187.9 5.4 %all_gather.31 = f32[256,128]{1,0:T(8,128)S(1)} all-gather(f32[64,128]{1,0:T(8,128)S(1)} %fusion.29), channel_id=1, replica_groups=mesh['prow'=4,'pcol'=8] {'prow'}, dimensions={0}, use_global_device_ids=true | all-gather | bytes 163840 | tf_op jit(solution)/shard_map/all_gather | solution.py:37
  195.4 5.6 %all_gather.32 = f32[256,128]{1,0:T(8,128)S(1)} all-gather(f32[64,128]{1,0:T(8,128)S(1)} %fusion.31), channel_id=1, replica_groups=mesh['prow'=4,'pcol'=8] {'prow'}, dimensions={0}, use_global_device_ids=true | all-gather | bytes 163840 | tf_op jit(solution)/shard_map/all_gather | solution.py:37
  203.1 5.4 %all_gather.33 = f32[256,128]{1,0:T(8,128)S(1)} all-gather(f32[64,128]{1,0:T(8,128)S(1)} %fusion.33), channel_id=1, replica_groups=mesh['prow'=4,'pcol'=8] {'prow'}, dimensions={0}, use_global_device_ids=true | all-gather | bytes 163840 | tf_op jit(solution)/shard_map/all_gather | solution.py:37
  210.7 5.4 %all_gather.34 = f32[256,128]{1,0:T(8,128)S(1)} all-gather(f32[64,128]{1,0:T(8,128)S(1)} %fusion.35), channel_id=1, replica_groups=mesh['prow'=4,'pcol'=8] {'prow'}, dimensions={0}, use_global_device_ids=true | all-gather | bytes 163840 | tf_op jit(solution)/shard_map/all_gather | solution.py:37
  216.1 1.3 constant_dynamic-update-slice_fusion.16
  218.2 5.4 %all_gather.35 = f32[256,128]{1,0:T(8,128)S(1)} all-gather(f32[64,128]{1,0:T(8,128)S(1)} %fusion.37), channel_id=1, replica_groups=mesh['prow'=4,'pcol'=8] {'prow'}, dimensions={0}, use_global_device_ids=true | all-gather | bytes 163840 | tf_op jit(solution)/shard_map/all_gather | solution.py:37
  (58 shorter events, 23.3 us)
Async XLA Ops:
  6.5 80.6 %all-gather.2.cloned.1.call-start = ((), (), s32[]{:S(2)}) async-start(), calls=%async_computation | async-start | bytes 4718592 | tf_op jit(solution)/shard_map/all_gather | solution.py:24
  7.3 154.9 %all-reduce.4.cloned.1.call-start = ((), (), s32[]{:S(2)}) async-start(), calls=%async_computation.1 | async-start | bytes 524288 | tf_op jit(solution)/shard_map/psum | solution.py:35
  7.3 11.2 %copy-start = (f32[16128,128]{1,0:T(8,128)S(1)}, f32[16128,128]{1,0:T(8,128)}, u32[]{:S(2)}) copy-start(f32[16128,128]{1,0:T(8,128)} %param.7) | copy-start | bytes 24772612
  7.3 51.6 %collective-permute-start = (f32[8,64,256]{2,1,0:T(8,128)}, f32[8,64,256]{2,1,0:T(8,128)S(1)}, u32[]{:S(2)}, u32[]{:S(2)}) collective-permute-start(f32[8,64,256]{2,1,0:T(8,128)} %param.9), channel_id=1, source_target_pairs={{0,8},{8,16},{16,24},{24,0},{1,9},{9,17},{17,25},{25,1},{2,10},{10... | collective-permute-start | bytes 1572872 | tf_op jit(solution)/shard_map/ppermute | solution.py:20
  58.9 10.3 %collective-permute-start.1 = (f32[8,64,256]{2,1,0:T(8,128)S(1)}, f32[8,64,256]{2,1,0:T(8,128)S(1)}, u32[]{:S(2)}, u32[]{:S(2)}) collective-permute-start(f32[8,64,256]{2,1,0:T(8,128)S(1)} %collective-permute-done), channel_id=1, source_target_pairs={{0,8},{8,16},{16,24},{24,0},{1,9},{9,17},{17,25},{25,1},{2,10},{10... | collective-permute-start | bytes 1572872 | tf_op jit(solution)/shard_map/ppermute | solution.py:20
  69.1 11.6 %copy-start.2 = (f32[8,64,256]{2,1,0:T(8,128)S(1)}, f32[8,64,256]{2,1,0:T(8,128)}, u32[]{:S(2)}) copy-start(f32[8,64,256]{2,1,0:T(8,128)} %param.9) | copy-start | bytes 1572868
  69.1 9.0 %collective-permute-start.2 = (f32[8,64,256]{2,1,0:T(8,128)S(1)}, f32[8,64,256]{2,1,0:T(8,128)S(1)}, u32[]{:S(2)}, u32[]{:S(2)}) collective-permute-start(f32[8,64,256]{2,1,0:T(8,128)S(1)} %collective-permute-done.1), channel_id=1, source_target_pairs={{0,8},{8,16},{16,24},{24,0},{1,9},{9,17},{17,25},{25,1},{2,10},{10... | collective-permute-start | bytes 1572872 | tf_op jit(solution)/shard_map/ppermute | solution.py:20
  79.0 83.1 %copy-start.3 = (f32[8,64,128]{2,1,0:T(8,128)S(1)}, f32[8,64,128]{2,1,0:T(8,128)}, u32[]{:S(2)}) copy-start(f32[8,64,128]{2,1,0:T(8,128)} %param.5) | copy-start | bytes 786436
  162.1 24.9 %copy-start.1 = (f32[8,64,2048]{2,1,0:T(8,128)S(1)}, f32[8,64,2048]{2,1,0:T(8,128)}, u32[]{:S(2)}) copy-start(f32[8,64,2048]{2,1,0:T(8,128)} %all-gather.2.cloned.1.call-done) | copy-start | bytes 12582916
  162.1 24.9 %copy-start.8 = (f32[64,128]{1,0:T(8,128)S(1)}, f32[64,128]{1,0:T(8,128)}, u32[]{:S(2)}) copy-start(f32[64,128]{1,0:T(8,128)} %get-tuple-element.8) | copy-start | bytes 98308
  163.1 31.5 %copy-start.7 = (f32[64,128]{1,0:T(8,128)S(1)}, f32[64,128]{1,0:T(8,128)}, u32[]{:S(2)}) copy-start(f32[64,128]{1,0:T(8,128)} %get-tuple-element.9) | copy-start | bytes 98308
  171.7 30.6 %copy-start.6 = (f32[64,128]{1,0:T(8,128)S(1)}, f32[64,128]{1,0:T(8,128)}, u32[]{:S(2)}) copy-start(f32[64,128]{1,0:T(8,128)} %get-tuple-element.10) | copy-start | bytes 98308
  180.3 29.6 %copy-start.5 = (f32[64,128]{1,0:T(8,128)S(1)}, f32[64,128]{1,0:T(8,128)}, u32[]{:S(2)}) copy-start(f32[64,128]{1,0:T(8,128)} %get-tuple-element.11) | copy-start | bytes 98308
  187.8 29.6 %copy-start.4 = (f32[64,128]{1,0:T(8,128)S(1)}, f32[64,128]{1,0:T(8,128)}, u32[]{:S(2)}) copy-start(f32[64,128]{1,0:T(8,128)} %get-tuple-element.12) | copy-start | bytes 98308
  225.1 0.7 copy-start.9
Sparse Core Ops, SparseCore 0:
  9.4 77.7 all-gather.1
  91.4 70.6 all-reduce.3
